TPU v7x, 512 devices: a whole 4x4x16 slice. The times are simulated.
512 devices in a mesh: section: 4 (over x), trial: 128 (over z, y, core).
Axes of the slice: x: 4, y: 4, z: 16, core: 2. Of those that a mesh axis runs over, the one named last changes fastest.
Arguments:
- spike_rates: bfloat16 [512, 256, 256], P(None, 'trial'), may hold values from -6 to 6
- first_preactivation: bfloat16 [1024, 256, 256], P('section', 'trial'), may hold values from -6 to 6
- second_preactivation: bfloat16 [1024, 256, 256], P('section', 'trial'), may hold values from -6 to 6
- output_gradient: bfloat16 [1024, 256, 256], P('section', 'trial'), may hold values from -0.29882812 to 0.29882812
- first_kernel: bfloat16 [3, 1024, 1024], P(None, None, 'section'), may hold values from -0.109375 to 0.109375
- second_kernel: bfloat16 [3, 1024, 1024], P(None, None, 'section'), may hold values from -0.109375 to 0.109375
- session_of: int32 [256], P('trial'), may hold values from 0 to 127, never falling along the last dimension, each value on 1 to 6 neighbouring positions
Outputs:
- readin_grad: bfloat16 [128, 512, 1024], P(None, 'trial', 'section')
Inputs may be any that keep to these rules, and one draw needn't show every extreme that they name: `session_of`: the trials of a session are consecutive; every session has 1 to 6 trials, and one has exactly 6.
All inputs are finite; a program needn't handle non-finite values.
Results may differ from a plain program's by a relative error of at most 0.017.
Values may be sent and summed in bfloat16 or wider, within the bound.
No kernel may reach another device: no remote copies, remote signals or barrier semaphores. Data moves between devices by JAX's collectives and lax.ppermute only.
A program may use at most 64 MiB of HBM per device.

v0:
```python
import math
import jax
import jax.numpy as jnp
from jax import lax
from jax.sharding import PartitionSpec as P

FIRST_DILATION = 32
SECOND_DILATION = 64
MOST = 6


def gelu_slope(preact):
    values = preact.astype(jnp.float32)
    normal_cdf = 0.5 * (1.0 + lax.erf(values * (1.0 / math.sqrt(2.0))))
    density = jnp.exp(-0.5 * values * values) * (1.0 / math.sqrt(2.0 * math.pi))
    return normal_cdf + values * density


def shift_ahead(values, offset):
    padding = [(0, 0)] * (values.ndim - 1) + [(0, offset)]
    return jnp.pad(values[..., offset:], padding)


def tap_sum(weights, flow_grad, spacing):
    running = None
    for kernel_tap in range(3):
        term_tap = lax.dot_general(
            weights[kernel_tap],
            flow_grad,
            (((1,), (0,)), ((), ())),
            preferred_element_type=jnp.float32,
        )
        if kernel_tap > 0:
            term_tap = shift_ahead(term_tap, kernel_tap * spacing)
        running = term_tap if running is None else running + term_tap
    return running


def layer_backprop(upstream, preact, turned, spacing):
    flow_grad = (upstream.astype(jnp.float32) * gelu_slope(preact)).astype(jnp.bfloat16)
    back_sum = tap_sum(turned, lax.all_gather(flow_grad, "section", axis=0, tiled=True), spacing)
    return (upstream.astype(jnp.float32) + back_sum).astype(jnp.bfloat16)


def body(
    spike_rates,
    first_preactivation,
    second_preactivation,
    output_gradient,
    first_kernel,
    second_kernel,
    session_of,
):
    first_flipped_kernel, second_flipped_kernel = (
        lax.all_to_all(first_kernel, "section", split_axis=1, concat_axis=2, tiled=True),
        lax.all_to_all(second_kernel, "section", split_axis=1, concat_axis=2, tiled=True),
    )
    upstream_gradient = layer_backprop(
        output_gradient, second_preactivation, second_flipped_kernel, SECOND_DILATION
    )
    input_gradient = layer_backprop(
        upstream_gradient, first_preactivation, first_flipped_kernel, FIRST_DILATION
    )
    trial_shards = lax.axis_size("trial")
    neurons, trials, steps_count = spike_rates.shape
    neuron_blocks = spike_rates.reshape(trial_shards, neurons // trial_shards, trials, steps_count)
    partials = jnp.einsum(
        "jbil,cil->jibc", neuron_blocks, input_gradient, preferred_element_type=jnp.float32
    )
    arrived = lax.all_to_all(
        partials.astype(jnp.bfloat16), "trial", split_axis=0, concat_axis=0, tiled=True
    ).astype(partials.dtype)
    every_id = lax.all_gather(session_of, "trial", axis=0, tiled=True)
    total_trials = every_id.shape[0]
    flat_parts = arrived.reshape(total_trials, -1)
    session_list = jnp.arange(trial_shards, dtype=jnp.int32)
    first_trial = jnp.sum((every_id[None, :] < session_list[:, None]).astype(jnp.int32), axis=1)

    def add_offset(offset, running):
        position = first_trial + offset
        clipped = jnp.minimum(position, total_trials - 1)
        rows_here = jnp.take(flat_parts, clipped, axis=0)
        valid = (position < total_trials) & (jnp.take(every_id, clipped, axis=0) == session_list)
        return running + jnp.where(valid[:, None], rows_here, 0.0)

    start_sums = jnp.zeros((trial_shards, flat_parts.shape[1]), jnp.float32)
    summed = lax.fori_loop(0, MOST, add_offset, start_sums)
    return summed.reshape(trial_shards, neurons // trial_shards, input_gradient.shape[0]).astype(
        jnp.bfloat16
    )


def solution(mesh):
    in_specs = (
        P(None, "trial", None),
        P("section", "trial", None),
        P("section", "trial", None),
        P("section", "trial", None),
        P(None, None, "section"),
        P(None, None, "section"),
        P("trial"),
    )
    out_specs = P(None, "trial", "section")
    return jax.shard_map(body, mesh=mesh, in_specs=in_specs, out_specs=out_specs, check_vma=False)
```

profile of v0, /device:TPU:8, one launch (start us, length us, event | category | flops | bytes accessed | tf_op | source)
XLA Modules:
  0.0 186.1 jit_solution(364001516441620479)
XLA Ops:
  6.5 0.0 copy-start
  6.5 0.0 all-gather.3.cloned.1.call-start
  6.5 1.2 copy.50
  7.8 1.1 copy.51
  8.9 1.0 fusion.14
  9.9 0.0 all-gather.3.cloned.1.call-update
  9.9 0.0 copy-done.3
  9.9 2.7 %copy.52 = bf16[3,1024,256]{2,0,1:T(4,128)(2,1)} copy(bf16[3,1024,256]{2,1,0:T(8,128)(2,1)S(1)} %copy-done.3) | data formatting | bytes 3145728 | tf_op args[5]
  12.6 4.4 %all-to-all-start = ((bf16[3,1024,256]{2,0,1:T(4,128)(2,1)}), bf16[3,1024,256]{2,0,1:T(4,128)(2,1)S(1)}, u32[]{:S(2)}, u32[]{:S(2)}) async-start(bf16[3,1024,256]{2,0,1:T(4,128)(2,1)} %copy.52), calls=%async_computation | async-start | bytes 4194304 | tf_op jit(solution)/shard_map/all_to_all | solution.py:56
  17.0 0.0 all-gather.5.cloned.1.call-start
  17.0 0.2 copy.54
  17.2 29.0 %all-to-all-done = bf16[3,1024,256]{2,0,1:T(4,128)(2,1)S(1)} async-done(((bf16[3,1024,256]{2,0,1:T(4,128)(2,1)}), bf16[3,1024,256]{2,0,1:T(4,128)(2,1)S(1)}, u32[]{:S(2)}, u32[]{:S(2)}) %all-to-all-start) | async-done | bytes 1572896 | tf_op jit(solution)/shard_map/all_to_all | solution.py:56
  46.2 1.5 copy.79
  47.7 0.5 fusion.34
  48.2 0.4 reshape.105
  48.6 0.4 reshape.106
  49.0 0.4 reshape.104
  49.4 6.2 %all-gather.3.cloned.1.call-done = bf16[1024,2,256]{0,2,1:T(8,128)(2,1)} async-done(((bf16[256,2,256]{0,2,1:T(8,128)(2,1)}), bf16[1024,2,256]{0,2,1:T(8,128)(2,1)}) %all-gather.3.cloned.1.call-update) | async-done | bytes 1048592 | tf_op jit(solution)/shard_map/all_gather | solution.py:41
  55.6 1.8 convolution_bitcast_fusion.4
  57.4 0.5 convolution_bitcast_fusion.3
  57.9 0.0 copy-start.4
  57.9 1.5 fusion.31
  59.4 0.0 all-gather.5.cloned.1.call-update
  59.4 0.0 copy-done.4
  59.4 1.4 copy.55
  60.8 31.6 %all_to_all.35 = bf16[3,1024,256]{2,0,1:T(4,128)(2,1)S(1)} all-to-all(bf16[3,1024,256]{2,0,1:T(4,128)(2,1)S(1)} %copy.55), channel_id=1, replica_groups=mesh['section'=4,'trial'=128] {'section'}, dimensions={1} | all-to-all | bytes 3145728 | tf_op jit(solution)/shard_map/all_to_all | solution.py:55
  92.3 0.2 copy.56
  92.6 0.1 fusion.33
  92.7 0.2 copy.59
  92.9 0.2 copy.61
  93.1 0.2 copy.57
  93.3 7.2 %all-gather.5.cloned.1.call-done = bf16[1024,2,256]{0,2,1:T(8,128)(2,1)} async-done(((bf16[256,2,256]{0,2,1:T(8,128)(2,1)}), bf16[1024,2,256]{0,2,1:T(8,128)(2,1)}) %all-gather.5.cloned.1.call-update) | async-done | bytes 1048592 | tf_op jit(solution)/shard_map/all_gather | solution.py:41
  100.5 1.8 convolution_bitcast_fusion.1
  102.3 0.4 convolution_bitcast_fusion
  102.8 2.0 %fusion.3 = bf16[128,2,4,256]{0,3,2,1:T(8,128)(2,1)S(1)} fusion(f32[256,2,256]{0,2,1:T(8,128)} %get-tuple-element.154, bf16[1024,2,256]{0,2,1:T(8,128)(2,1)S(1)} %copy-done.1, bf16[256,1024,1]{0,1,2:T(8,128)(2,1)S(1)} %bitcast.90, bf16[128,4,2,256]{3,2,1,0:T(2,128)(2,1)S(1)} %bitcast.84, f32[256,2,192]{0,2,1:T(8,128)S(1)} %slice.59, ...), kind=kOutput, calls=%fused_computation.13 | convolution fusion | flops 403439616 | bytes 3997696 | tf_op jit(solution)/shard_map/jbil,cil->jibc/dot_general | solution.py:67
  104.8 0.0 copy-start.6
  104.8 1.2 copy.65
  106.0 19.0 %all-to-all-start.2 = ((bf16[128,2,4,256]{3,2,1,0:T(4,128)(2,1)}), bf16[128,2,4,256]{3,2,1,0:T(4,128)(2,1)S(1)}, u32[]{:S(2)}, u32[]{:S(2)}) async-start(bf16[128,2,4,256]{3,2,1,0:T(4,128)(2,1)} %copy.65), calls=%async_computation.2 | async-start | bytes 1048576 | tf_op jit(solution)/shard_map/all_to_all | solution.py:70
  125.0 1.2 dynamic-slice
  126.8 0.2 dynamic-update-slice
  127.1 37.2 %all-reduce.4 = s32[256]{0:T(256)S(1)} all-reduce(s32[256]{0:T(256)S(1)} %dynamic-update-slice), channel_id=1, replica_groups=mesh['section'=4,'trial'=128] {'trial'}, use_global_device_ids=true, to_apply=%add.4 | all-reduce | flops 256 | bytes 2048
  164.3 0.1 convert_reduce_fusion
  164.4 0.0 all-to-all-done.2
  164.4 0.1 copy.75
  164.5 13.8 %while.14 = (s32[]{:T(128)}, f32[128,1024]{1,0:T(8,128)S(1)}, s32[128]{0:T(128)S(1)}, s32[256]{0:T(256)S(1)}, f32[256,1024]{1,0:T(8,128)S(1)}, /*index=5*/s32[]{:T(128)}, s32[]{:T(128)}) while((s32[]{:T(128)}, f32[128,1024]{1,0:T(8,128)S(1)}, s32[128]{0:T(128)S(1)}, s32[256]{0:T(256)S(1)}, f32[256,1024]{1,0:T(8,128)S(1)}, ...), condition=%wide.region_2.3_spmd.clone, body=%wide.region_1.2_spmd.clone.sunk | while | flops 527491 | bytes 2630751 | solution.py:87
  164.6 1.3 gather_fusion.1
  165.9 0.8 gather_fusion
  166.7 0.2 select_add_fusion.2
  166.9 1.3 gather_fusion.1
  168.1 0.8 gather_fusion
  169.0 0.2 select_add_fusion.2
  169.2 1.3 gather_fusion.1
  170.4 0.8 gather_fusion
  171.3 0.2 select_add_fusion.2
  171.5 1.3 gather_fusion.1
  172.7 0.8 gather_fusion
  173.6 0.2 select_add_fusion.2
  173.7 1.3 gather_fusion.1
  175.0 0.8 gather_fusion
  175.8 0.2 select_add_fusion.2
  176.0 1.3 gather_fusion.1
  177.3 0.8 gather_fusion
  178.1 0.2 select_add_fusion.2
  178.3 0.9 convert_element_type.61
  (34 shorter events, 0.3 us)
Async XLA Ops:
  6.5 96.3 %copy-start = (bf16[512,2,256]{2,1,0:T(2,128)(2,1)S(1)}, bf16[512,2,256]{2,1,0:T(2,128)(2,1)}, u32[]{:S(2)}) copy-start(bf16[512,2,256]{2,1,0:T(2,128)(2,1)} %param.9) | copy-start | bytes 1572868
  6.5 3.4 %copy-start.3 = (bf16[3,1024,256]{2,1,0:T(8,128)(2,1)S(1)}, bf16[3,1024,256]{2,1,0:T(8,128)(2,1)}, u32[]{:S(2)}) copy-start(bf16[3,1024,256]{2,1,0:T(8,128)(2,1)} %param.14) | copy-start | bytes 4718596
  6.5 49.0 %all-gather.3.cloned.1.call-start = ((), (), s32[]{:S(2)}) async-start(), calls=%async_computation.3 | async-start | bytes 1310720 | tf_op jit(solution)/shard_map/all_gather | solution.py:41
  12.6 4.4 %copy-start.5 = (bf16[256,2,256]{2,1,0:T(2,128)(2,1)S(1)}, bf16[256,2,256]{2,1,0:T(2,128)(2,1)}, u32[]{:S(2)}) copy-start(bf16[256,2,256]{2,1,0:T(2,128)(2,1)} %param.10) | copy-start | bytes 786436
  12.6 33.6 %all-to-all-start = ((bf16[3,1024,256]{2,0,1:T(4,128)(2,1)}), bf16[3,1024,256]{2,0,1:T(4,128)(2,1)S(1)}, u32[]{:S(2)}, u32[]{:S(2)}) async-start(bf16[3,1024,256]{2,0,1:T(4,128)(2,1)} %copy.52), calls=%async_computation | async-start | bytes 4194304 | tf_op jit(solution)/shard_map/all_to_all | solution.py:56
  17.0 83.5 %all-gather.5.cloned.1.call-start = ((), (), s32[]{:S(2)}) async-start(), calls=%async_computation.4 | async-start | bytes 1310720 | tf_op jit(solution)/shard_map/all_gather | solution.py:41
  55.6 1.8 copy-start.2
  57.9 1.5 copy-start.4
  100.5 1.8 copy-start.1
  104.8 22.1 %copy-start.6 = (s32[2]{0:T(128)S(1)}, s32[2]{0:T(128)}, u32[]{:S(2)}) copy-start(s32[2]{0:T(128)} %param.15) | copy-start | bytes 28
  106.0 58.4 %all-to-all-start.2 = ((bf16[128,2,4,256]{3,2,1,0:T(4,128)(2,1)}), bf16[128,2,4,256]{3,2,1,0:T(4,128)(2,1)S(1)}, u32[]{:S(2)}, u32[]{:S(2)}) async-start(bf16[128,2,4,256]{3,2,1,0:T(4,128)(2,1)} %copy.65), calls=%async_computation.2 | async-start | bytes 1048576 | tf_op jit(solution)/shard_map/all_to_all | solution.py:70
Sparse Core Ops, SparseCore 0:
  10.0 45.5 all-gather.2
  59.5 40.9 all-gather.4
where the time goes:
time: 187 us; the launch traced here: 186 us
  blocking collectives  68.8 us (37%)
  waiting for transfers between devices  42.5 us (23%)
  local copies, waits for them, and re-layouts  26.8 us (14%)
  starting transfers between devices  23.4 us (13%)
  between operations  14.2 us (8%)
  matrix products  7.88 us (4%)
  other arithmetic  2.14 us (1%)
    unnamed x1, blocking collectives  37.2 us
    all_to_all x1, blocking collectives, body(): lax.all_to_all(first_kernel, 'section', split_axis=1, concat_axis=2, tile...  31.6 us
    all_to_all x1, waiting for transfers between devices, body(): lax.all_to_all(second_kernel, 'section', split_axis=1, concat_axis=2, til...  29 us
    all_to_all x1, starting transfers between devices, body(): lax.all_to_all(partials.astype(jnp.bfloat16), 'trial', split_axis=0, conc...  19 us
    all_gather x2, waiting for transfers between devices, layer_backprop(): lax.all_gather(flow_grad, 'section', axis=0, tiled=True)  13.4 us
    unnamed x23, local copies, waits for them, and re-layouts  8.19 us
    gather x6, local copies, waits for them, and re-layouts, add_offset(): jnp.take(every_id, clipped, axis=0) == session_list  7.59 us
    dot_general x5, matrix products, tap_sum(): lax.dot_general(weights[kernel_tap], flow_grad, (((1,), (0,)), ((), ())),...  5.91 us
  transfers between devices with their start and end apart: 4, of which 3 were waited for; matrix products, arithmetic and copies ran while one was open for 5% of the time, Pallas kernels for 0%

commit v1 on v0

--- a/solution.py
+++ b/solution.py
@@ -7,6 +7,12 @@
 FIRST_DILATION = 32
 SECOND_DILATION = 64
 MOST = 6
+
+
+def exchange_blocks(value, axis, split, join):
+    cells = jnp.split(value, lax.axis_size(axis), axis=split)
+    incoming = lax.all_to_all(jnp.stack(cells), axis, 0, 0)
+    return jnp.concatenate(incoming, axis=join)
 
 
 def gelu_slope(preact):
@@ -53,7 +59,7 @@
 ):
     first_flipped_kernel, second_flipped_kernel = (
         lax.all_to_all(first_kernel, "section", split_axis=1, concat_axis=2, tiled=True),
-        lax.all_to_all(second_kernel, "section", split_axis=1, concat_axis=2, tiled=True),
+        exchange_blocks(second_kernel, "section", 1, 2),
     )
     upstream_gradient = layer_backprop(
         output_gradient, second_preactivation, second_flipped_kernel, SECOND_DILATION

time: 187 us -> 177 us (0.947)
  waiting for transfers between devices: 42.5 us -> 8.75 us
  blocking collectives: 68.8 us -> 97.4 us
  starting transfers between devices: 23.4 us -> 19.6 us
  local copies, waits for them, and re-layouts: 26.8 us -> 23.8 us
    all_to_all x1 -> x0, waiting for transfers between devices: 29 us -> none  [body(): lax.all_to_all(second_kernel, 'section', split_axis=1, concat_axis=2, til...]
    all_to_all x0 -> x1, blocking collectives: none -> 24.8 us  [exchange_blocks(): incoming = lax.all_to_all(jnp.stack(cells), axis, 0, 0)]
    unnamed x23 -> x19, local copies, waits for them, and re-layouts: 8.19 us -> 3.08 us
    all_gather x2, waiting for transfers between devices: 13.4 us -> 8.72 us  [layer_backprop(): lax.all_gather(flow_grad, 'section', axis=0, tiled=True)]
    all_to_all x1 -> x0, starting transfers between devices: 4.42 us -> none  [body(): lax.all_to_all(second_kernel, 'section', split_axis=1, concat_axis=2, til...]
    all_to_all x1, blocking collectives: 31.6 us -> 35.6 us  [body(): lax.all_to_all(first_kernel, 'section', split_axis=1, concat_axis=2, tile...]
  transfers between devices with their start and end apart: 4 -> 3, of which waited for: 3 -> 2; matrix products, arithmetic and copies ran while one was open for 5% -> 5% of each run, Pallas kernels for 0% -> 0%
where the time goes in v1:
time: 177 us; the launch traced here: 176 us
  blocking collectives  97.4 us (55%)
  local copies, waits for them, and re-layouts  23.8 us (13%)
  starting transfers between devices  19.6 us (11%)
  between operations  14.3 us (8%)
  waiting for transfers between devices  8.75 us (5%)
  matrix products  8.48 us (5%)
  other arithmetic  3.43 us (2%)
    unnamed x1, blocking collectives  37 us
    all_to_all x1, blocking collectives, body(): lax.all_to_all(first_kernel, 'section', split_axis=1, concat_axis=2, tile...  35.6 us
    all_to_all x1, blocking collectives, exchange_blocks(): incoming = lax.all_to_all(jnp.stack(cells), axis, 0, 0)  24.8 us
    all_to_all x1, starting transfers between devices, body(): lax.all_to_all(partials.astype(jnp.bfloat16), 'trial', split_axis=0, conc...  19.6 us
    all_gather x2, waiting for transfers between devices, layer_backprop(): lax.all_gather(flow_grad, 'section', axis=0, tiled=True)  8.72 us
    gather x6, local copies, waits for them, and re-layouts, add_offset(): jnp.take(every_id, clipped, axis=0) == session_list  7.59 us
    dot_general x5, matrix products, tap_sum(): lax.dot_general(weights[kernel_tap], flow_grad, (((1,), (0,)), ((), ())),...  5.88 us
    gather x6, local copies, waits for them, and re-layouts, add_offset(): rows_here = jnp.take(flat_parts, clipped, axis=0)  4.8 us
  transfers between devices with their start and end apart: 3, of which 2 were waited for; matrix products, arithmetic and copies ran while one was open for 5% of the time, Pallas kernels for 0%

profile of v1, /device:TPU:8, one launch (start us, length us, event | category | flops | bytes accessed | tf_op | source)
XLA Modules:
  0.0 176.2 jit_solution(1094010181891371230)
XLA Ops:
  6.5 0.0 copy-start
  6.5 2.0 %fusion.15 = bf16[256,2,256]{2,0,1:T(8,128)(2,1)} fusion(bf16[256,2,256]{2,1,0:T(2,128)(2,1)} %param.11, bf16[256,2,256]{2,1,0:T(2,128)(2,1)} %param.12), kind=kLoop, calls=%fused_computation.38 | loop fusion | flops 1572864 | bytes 786432 | tf_op jit(solution)/shard_map/convert_element_type | solution.py:46
  8.6 0.0 all-gather.3.cloned.1.call-update
  8.6 0.0 all-gather.5.cloned.1.call-start
  8.7 1.5 slice_bitcast_fusion.3
  10.1 0.2 pad_maximum_fusion
  10.3 24.8 %all_to_all.25 = bf16[4,3,256,256]{3,2,1,0:T(8,128)(2,1)S(1)} all-to-all(bf16[4,3,256,256]{3,2,1,0:T(8,128)(2,1)S(1)} %pad_maximum_fusion), channel_id=1, replica_groups=mesh['section'=4,'trial'=128] {'section'}, dimensions={0} | all-to-all | bytes 3145728 | tf_op jit(solution)/shard_map/all_to_all | solution.py:14
  35.2 0.1 fusion.37
  35.3 0.4 copy.76
  35.7 0.4 reshape.110
  36.1 0.4 copy.79
  36.5 0.4 reshape.111
  36.8 0.4 copy.74
  37.3 0.4 reshape.109
  37.6 0.0 copy-start.3
  37.6 0.0 copy-start.5
  37.7 8.0 %all-gather.3.cloned.1.call-done = bf16[1024,2,256]{2,0,1:T(8,128)(2,1)} async-done(((bf16[256,2,256]{2,0,1:T(8,128)(2,1)}), bf16[1024,2,256]{2,0,1:T(8,128)(2,1)}) %all-gather.3.cloned.1.call-update) | async-done | bytes 1048592 | tf_op jit(solution)/shard_map/all_gather | solution.py:47
  45.7 1.9 %fusion.13 = f32[256,2,192]{2,0,1:T(8,128)S(1)} fusion(bf16[256,1024,1]{1,0,2:T(8,128)(2,1)S(1)} %reshape.110, bf16[1024,2,256]{2,0,1:T(8,128)(2,1)} %all-gather.3.cloned.1.call-done), kind=kOutput, calls=%fused_computation.27 | convolution fusion | flops 201326592 | bytes 1966080 | tf_op jit(solution)/shard_map/dot_general | solution.py:33
  47.6 0.3 fusion.29
  47.9 0.0 copy-start.2
  47.9 1.5 fusion.34
  49.4 0.0 all-gather.5.cloned.1.call-update
  49.4 1.4 copy.81
  50.8 35.6 %all_to_all.26 = bf16[3,1024,256]{2,0,1:T(4,128)(2,1)S(1)} all-to-all(bf16[3,1024,256]{2,0,1:T(4,128)(2,1)S(1)} %copy.81), channel_id=1, replica_groups=mesh['section'=4,'trial'=128] {'section'}, dimensions={1} | all-to-all | bytes 3145728 | tf_op jit(solution)/shard_map/all_to_all | solution.py:61
  86.3 0.2 copy.82
  86.6 0.1 fusion.36
  86.7 0.2 copy.87
  86.9 0.2 copy.91
  87.1 0.2 copy.83
  87.3 0.7 all-gather.5.cloned.1.call-done
  88.0 1.8 %convolution_bitcast_fusion.1 = f32[256,2,256]{2,0,1:T(8,128)S(1)} fusion(bf16[1024,2,256]{2,0,1:T(8,128)(2,1)} %all-gather.5.cloned.1.call-done, bf16[256,1024,1]{0,1,2:T(8,128)(2,1)S(1)} %bitcast.77), kind=kOutput, calls=%fused_computation.17 | convolution fusion | flops 268435456 | bytes 2097152 | tf_op jit(solution)/shard_map/dot_general | solution.py:33
  89.8 0.2 slice.59
  90.0 0.0 copy-done.1
  90.0 0.5 convolution_bitcast_fusion
  90.5 0.2 slice.61
  90.7 2.6 %fusion.4 = bf16[128,2,4,256]{0,3,2,1:T(8,128)(2,1)} fusion(f32[256,2,256]{2,0,1:T(8,128)} %get-tuple-element.158, bf16[1024,2,256]{2,0,1:T(8,128)(2,1)S(1)} %copy-done.1, bf16[256,1024,1]{0,1,2:T(8,128)(2,1)S(1)} %bitcast.78, bf16[128,4,2,256]{3,2,1,0:T(2,128)(2,1)S(1)} %bitcast.71, f32[256,2,192]{2,0,1:T(8,128)S(1)} %slice.61, f32[256,2,224]{2,0,1:T(8,128)S(1)} %slice.59), kind=kOutput, calls=%fused_computation.15 | convolution fusion | flops 403439616 | bytes 3997696 | tf_op jit(solution)/shard_map/jbil,cil->jibc/dot_general | solution.py:73
  93.3 2.2 %copy.96 = bf16[128,2,4,256]{3,2,1,0:T(4,128)(2,1)} copy(bf16[128,2,4,256]{0,3,2,1:T(8,128)(2,1)} %fusion.4) | data formatting | bytes 1048576 | tf_op jit(solution)/shard_map/convert_element_type | solution.py:77
  95.5 19.6 %all-to-all-start.2 = ((bf16[128,2,4,256]{3,2,1,0:T(4,128)(2,1)}), bf16[128,2,4,256]{3,2,1,0:T(4,128)(2,1)S(1)}, u32[]{:S(2)}, u32[]{:S(2)}) async-start(bf16[128,2,4,256]{3,2,1,0:T(4,128)(2,1)} %copy.96), calls=%async_computation.2 | async-start | bytes 1048576 | tf_op jit(solution)/shard_map/all_to_all | solution.py:76
  115.1 1.3 dynamic-slice
  117.1 0.2 dynamic-update-slice
  117.4 37.0 %all-reduce.4 = s32[256]{0:T(256)S(1)} all-reduce(s32[256]{0:T(256)S(1)} %dynamic-update-slice), channel_id=1, replica_groups=mesh['section'=4,'trial'=128] {'trial'}, use_global_device_ids=true, to_apply=%add.4 | all-reduce | flops 256 | bytes 2048
  154.4 0.1 convert_reduce_fusion
  154.5 0.0 all-to-all-done.2
  154.5 0.1 copy.112
  154.6 13.8 %while.14 = (s32[]{:T(128)}, f32[128,1024]{1,0:T(8,128)S(1)}, s32[128]{0:T(128)S(1)}, s32[256]{0:T(256)S(1)}, f32[256,1024]{1,0:T(8,128)S(1)}, /*index=5*/s32[]{:T(128)}, s32[]{:T(128)}) while((s32[]{:T(128)}, f32[128,1024]{1,0:T(8,128)S(1)}, s32[128]{0:T(128)S(1)}, s32[256]{0:T(256)S(1)}, f32[256,1024]{1,0:T(8,128)S(1)}, ...), condition=%wide.region_2.3_spmd.clone, body=%wide.region_1.2_spmd.clone.sunk | while | flops 527491 | bytes 2630751 | solution.py:93
  154.7 1.3 gather_fusion.1
  156.0 0.8 gather_fusion
  156.8 0.2 select_add_fusion.2
  157.0 1.3 gather_fusion.1
  158.3 0.8 gather_fusion
  159.1 0.2 select_add_fusion.2
  159.3 1.3 gather_fusion.1
  160.6 0.8 gather_fusion
  161.4 0.2 select_add_fusion.2
  161.6 1.3 gather_fusion.1
  162.9 0.8 gather_fusion
  163.7 0.2 select_add_fusion.2
  163.9 1.3 gather_fusion.1
  165.2 0.8 gather_fusion
  166.0 0.2 select_add_fusion.2
  166.2 1.3 gather_fusion.1
  167.5 0.8 gather_fusion
  168.3 0.2 select_add_fusion.2
  168.5 0.9 convert_element_type.61
  (31 shorter events, 0.2 us)
Async XLA Ops:
  6.5 84.1 %copy-start = (bf16[512,2,256]{2,1,0:T(2,128)(2,1)S(1)}, bf16[512,2,256]{2,1,0:T(2,128)(2,1)}, u32[]{:S(2)}) copy-start(bf16[512,2,256]{2,1,0:T(2,128)(2,1)} %param.9) | copy-start | bytes 1572868
  6.5 39.2 %all-gather.3.cloned.1.call-start = ((), (), s32[]{:S(2)}) async-start(), calls=%async_computation.3 | async-start | bytes 1310720 | tf_op jit(solution)/shard_map/all_gather | solution.py:47
  8.6 79.4 %all-gather.5.cloned.1.call-start = ((), (), s32[]{:S(2)}) async-start(), calls=%async_computation.4 | async-start | bytes 1310720 | tf_op jit(solution)/shard_map/all_gather | solution.py:47
  37.6 10.2 %copy-start.3 = (bf16[256,2,256]{2,1,0:T(2,128)(2,1)S(1)}, bf16[256,2,256]{2,1,0:T(2,128)(2,1)}, u32[]{:S(2)}) copy-start(bf16[256,2,256]{2,1,0:T(2,128)(2,1)} %param.12) | copy-start | bytes 786436
  37.6 10.2 %copy-start.5 = (bf16[256,2,256]{2,1,0:T(2,128)(2,1)S(1)}, bf16[256,2,256]{2,1,0:T(2,128)(2,1)}, u32[]{:S(2)}) copy-start(bf16[256,2,256]{2,1,0:T(2,128)(2,1)} %param.10) | copy-start | bytes 786436
  45.7 1.9 %copy-start.4 = (bf16[1024,2,256]{2,0,1:T(8,128)(2,1)S(1)}, bf16[1024,2,256]{2,0,1:T(8,128)(2,1)}, u32[]{:S(2)}) copy-start(bf16[1024,2,256]{2,0,1:T(8,128)(2,1)} %all-gather.3.cloned.1.call-done) | copy-start | bytes 3145732
  47.9 1.5 copy-start.2
  88.0 2.0 %copy-start.1 = (bf16[1024,2,256]{2,0,1:T(8,128)(2,1)S(1)}, bf16[1024,2,256]{2,0,1:T(8,128)(2,1)}, u32[]{:S(2)}) copy-start(bf16[1024,2,256]{2,0,1:T(8,128)(2,1)} %all-gather.5.cloned.1.call-done) | copy-start | bytes 3145732
  93.3 23.8 %copy-start.6 = (s32[2]{0:T(128)S(1)}, s32[2]{0:T(128)}, u32[]{:S(2)}) copy-start(s32[2]{0:T(128)} %param.15) | copy-start | bytes 28
  95.5 59.0 %all-to-all-start.2 = ((bf16[128,2,4,256]{3,2,1,0:T(4,128)(2,1)}), bf16[128,2,4,256]{3,2,1,0:T(4,128)(2,1)S(1)}, u32[]{:S(2)}, u32[]{:S(2)}) async-start(bf16[128,2,4,256]{3,2,1,0:T(4,128)(2,1)} %copy.96), calls=%async_computation.2 | async-start | bytes 1048576 | tf_op jit(solution)/shard_map/all_to_all | solution.py:76
Sparse Core Ops, SparseCore 0:
  9.5 36.1 all-gather.2
  49.5 38.4 all-gather.4
